TPU v7x, 32 devices: a whole 2x2x4 slice. The times are simulated.
32 devices in a mesh: dp: 16 (over z, y, core), tensor: 2 (over x).
Axes of the slice: x: 2, y: 2, z: 4, core: 2. Of those that a mesh axis runs over, the one named last changes fastest.
Arguments:
- residual_in: float32 [8192, 1024], P(('dp', 'tensor')), may hold values from -6 to 6
- out_cotangent: float32 [8192, 1024], P(('dp', 'tensor')), may hold values from -6 to 6
- seq_lengths: int32 [4], replicated, may hold values from 1 to 4096, 8192 in all
- qkv_weight: float32 [1024, 3072], P('dp', 'tensor'), may hold values from -1 to 1
- out_weight: float32 [1024, 1024], P('tensor', 'dp'), may hold values from -2 to 2
- in_weight: float32 [1024, 2, 2624], P('dp', None, 'tensor'), may hold values from -0.1875 to 0.1875
- down_weight: float32 [2624, 1024], P('tensor', 'dp'), may hold values from -0.125 to 0.125
- norm_gains: float32 [2, 1024], replicated, may hold values from 0.5 to 1.5
- qkv_moments: float32 [2, 1024, 3072], P(None, 'dp', 'tensor'), may hold values from -8192 to 8192, as said below
- out_moments: float32 [2, 1024, 1024], P(None, 'tensor', 'dp'), may hold values from -8192 to 8192, as said below
- in_moments: float32 [2, 1024, 2, 2624], P(None, 'dp', None, 'tensor'), may hold values from -8192 to 8192, as said below
- down_moments: float32 [2, 2624, 1024], P(None, 'tensor', 'dp'), may hold values from -8192 to 8192, as said below
- gain_moments: float32 [2, 2, 1024], replicated, may hold values from -8192 to 8192, as said below
Outputs:
- block_out: float32 [8192, 1024], P(('dp', 'tensor'))
- residual_grad: float32 [8192, 1024], P(('dp', 'tensor'))
- qkv_grad: float32 [1024, 3072], P('dp', 'tensor')
- out_weight_grad: float32 [1024, 1024], P('tensor', 'dp')
- in_grad: float32 [1024, 2, 2624], P('dp', None, 'tensor')
- down_grad: float32 [2624, 1024], P('tensor', 'dp')
- gains_grad: float32 [2, 1024], replicated
- new_qkv: float32 [1024, 3072], P('dp', 'tensor')
- new_out: float32 [1024, 1024], P('tensor', 'dp')
- new_in: float32 [1024, 2, 2624], P('dp', None, 'tensor')
- new_down: float32 [2624, 1024], P('tensor', 'dp')
- new_gains: float32 [2, 1024], replicated
- new_qkv_moments: float32 [2, 1024, 3072], P(None, 'dp', 'tensor')
- new_out_moments: float32 [2, 1024, 1024], P(None, 'tensor', 'dp')
- new_in_moments: float32 [2, 1024, 2, 2624], P(None, 'dp', None, 'tensor')
- new_down_moments: float32 [2, 2624, 1024], P(None, 'tensor', 'dp')
- new_gain_moments: float32 [2, 2, 1024], replicated
Inputs may be any that keep to these rules, and one draw needn't show every extreme that they name: `seq_lengths`: the lengths sum to 8192; the longest is exactly 4096. `qkv_moments`: index 0 is the first moment, index 1 the second moment, which is positive. `out_moments`: index 0 is the first moment, index 1 the second moment, which is positive. `in_moments`: index 0 is the first moment, index 1 the second moment, which is positive. `down_moments`: index 0 is the first moment, index 1 the second moment, which is positive. `gain_moments`: index 0 is the first moment, index 1 the second moment, which is positive.
All inputs are finite; a program needn't handle non-finite values.
Results may differ from a plain program's by a relative error of at most 0.019.
Values may be sent and summed in bfloat16 or wider, within the bound.
A program may use at most 128 MiB of HBM per device.

v0:
```python
import math
import jax
import jax.numpy as jnp
from jax import lax
from jax.sharding import PartitionSpec as P

HD = 64
HALF_WIN = 64
STEP = 3
NORM_EPS = 1e-05
ROPE_BASE = 10000.0
BETA_ONE = 0.9
BETA_TWO = 0.999
ADAM_EPS = 1e-08
LEARN_RATE = 0.005
DECAY_RATE = 0.1
MASKED = -1e30


def padded(value, sides, width):
    for axis, dim in sides:
        size, length = (lax.axis_size(axis), value.shape[dim])
        up = [(i, (i + 1) % size) for i in range(size - 1)]
        down = [(j, i) for i, j in up]
        last = lax.slice_in_dim(value, length - width, length, axis=dim)
        first = lax.slice_in_dim(value, 0, width, axis=dim)
        before = lax.ppermute(last, axis, up)
        after = lax.ppermute(first, axis, down)
        value = jnp.concatenate([before, value, after], axis=dim)
    return value


def norm_forward(rows, gain):
    row_mean = jnp.mean(rows, axis=-1, keepdims=True)
    centered = rows - row_mean
    inv_std = lax.rsqrt(jnp.mean(centered * centered, axis=-1, keepdims=True) + NORM_EPS)
    normed = centered * inv_std
    return (normed, inv_std, normed * gain)


def norm_backward(grad_out, normed, inv_std, gain):
    scaled = grad_out * gain
    grad_rows = inv_std * (
        scaled
        - jnp.mean(scaled, axis=-1, keepdims=True)
        - normed * jnp.mean(scaled * normed, axis=-1, keepdims=True)
    )
    return (grad_rows, jnp.sum(grad_out * normed, axis=0))


def seq_coords(seq_lengths, places):
    seq_ends = jnp.cumsum(seq_lengths, dtype=jnp.int32)
    passed = (seq_ends[None, :] <= places[:, None]).astype(jnp.int32)
    seq_ids = jnp.sum(passed, axis=1, dtype=jnp.int32)
    seq_start = jnp.sum(passed * seq_lengths[None, :], axis=1, dtype=jnp.int32)
    return (seq_ids, places - seq_start)


def rotary_tables(offsets, head_dim):
    half_dim = head_dim // 2
    inv_freq = ROPE_BASE ** (-2.0 * jnp.arange(half_dim).astype(jnp.float32) / head_dim)
    angles = offsets.astype(jnp.float32)[:, None] * inv_freq[None, :]
    cos_table = jnp.cos(angles)
    sin_table = jnp.sin(angles)
    return (
        jnp.concatenate([cos_table, cos_table], axis=-1),
        jnp.concatenate([sin_table, sin_table], axis=-1),
    )


def rotate(feats, cos_table, sin_table):
    half_dim = feats.shape[-1] // 2
    turned = jnp.concatenate([-feats[..., half_dim:], feats[..., :half_dim]], axis=-1)
    return feats * cos_table[:, None, :] + turned * sin_table[:, None, :]


def unrotate(grads, cos_table, sin_table):
    half_dim = grads.shape[-1] // 2
    spun = grads * sin_table[:, None, :]
    back = jnp.concatenate([spun[..., half_dim:], -spun[..., :half_dim]], axis=-1)
    return grads * cos_table[:, None, :] + back


def gelu_parts(pre_act):
    normal_cdf = 0.5 * (1.0 + lax.erf(pre_act * (1.0 / math.sqrt(2.0))))
    density = jnp.exp(-0.5 * pre_act * pre_act) * (1.0 / math.sqrt(2.0 * math.pi))
    return (pre_act * normal_cdf, normal_cdf + pre_act * density)


def block_mask(query_ids, key_ids, reach):
    query_count = query_ids.shape[0]
    key_count = key_ids.shape[0]
    distance = (
        jnp.arange(key_count, dtype=jnp.int32)[None, :]
        - reach
        - jnp.arange(query_count, dtype=jnp.int32)[:, None]
    )
    return (query_ids[:, None] == key_ids[None, :]) & (jnp.abs(distance) <= reach)


def block_scores(query_rows, key_rows, allowed):
    score_scale = 1.0 / math.sqrt(query_rows.shape[-1])
    scores = (
        jnp.einsum("qhe,khe->hqk", query_rows, key_rows, preferred_element_type=jnp.float32)
        * score_scale
    )
    return jnp.where(allowed[None, :, :], scores, MASKED)


def block_forward(query_rows, key_rows, value_rows, allowed):
    scores = block_scores(query_rows, key_rows, allowed)
    row_max = jnp.max(scores, axis=-1, keepdims=True)
    log_norm = row_max + jnp.log(jnp.sum(jnp.exp(scores - row_max), axis=-1, keepdims=True))
    attn_probs = jnp.exp(scores - log_norm).astype(jnp.bfloat16)
    mixed = jnp.einsum("hqk,khe->qhe", attn_probs, value_rows, preferred_element_type=jnp.float32)
    return (mixed.astype(jnp.bfloat16), log_norm[..., 0])


def block_backward(query_rows, key_rows, value_rows, allowed, log_norm, grad_rows, deltas):
    score_scale = 1.0 / math.sqrt(query_rows.shape[-1])
    scores = block_scores(query_rows, key_rows, allowed)
    probs_full = jnp.exp(scores - log_norm[..., None])
    grad_probs = jnp.einsum(
        "qhe,khe->hqk", grad_rows, value_rows, preferred_element_type=jnp.float32
    )
    grad_scores = (probs_full * (grad_probs - jnp.transpose(deltas)[:, :, None])).astype(
        jnp.bfloat16
    )
    attn_probs = probs_full.astype(jnp.bfloat16)
    grad_queries = (
        jnp.einsum("hqk,khe->qhe", grad_scores, key_rows, preferred_element_type=jnp.float32)
        * score_scale
    )
    grad_keys = (
        jnp.einsum("hqk,qhe->khe", grad_scores, query_rows, preferred_element_type=jnp.float32)
        * score_scale
    )
    grad_values = jnp.einsum(
        "hqk,qhe->khe", attn_probs, grad_rows, preferred_element_type=jnp.float32
    )
    return (grad_queries, grad_keys, grad_values)


def product_rows(matrix, weight, contract_dim):
    return lax.dot_general(
        matrix, weight, (((1,), (contract_dim,)), ((), ())), preferred_element_type=jnp.float32
    )


def across_rows(left, right):
    return lax.dot_general(
        left, right, (((0,), (0,)), ((), ())), preferred_element_type=jnp.float32
    )


def against_cols(left, right):
    return lax.dot_general(
        left, right, (((1,), (1,)), ((), ())), preferred_element_type=jnp.float32
    )


def adam_update(weight, moments, grad, decay):
    first_moment = BETA_ONE * moments[0] + (1.0 - BETA_ONE) * grad
    second_moment = BETA_TWO * moments[1] + (1.0 - BETA_TWO) * grad * grad
    first_hat = first_moment / (1.0 - BETA_ONE**STEP)
    second_hat = second_moment / (1.0 - BETA_TWO**STEP)
    new_weight = weight - LEARN_RATE * (
        first_hat / (jnp.sqrt(second_hat) + ADAM_EPS) + decay * weight
    )
    return (new_weight, jnp.stack([first_moment, second_moment]))


def local(
    residual_in,
    out_cotangent,
    seq_lengths,
    qkv_weight,
    out_weight,
    in_weight,
    down_weight,
    norm_gains,
    qkv_moments,
    out_moments,
    in_moments,
    down_moments,
    gain_moments,
):
    tensor_count = lax.axis_size("tensor")
    data_count = lax.axis_size("dp")
    local_rows = residual_in.shape[0]
    seq_rows = local_rows * tensor_count
    reach = HALF_WIN
    block_rows = min(512, seq_rows)
    span = block_rows + 2 * reach
    qkv_full, out_full, in_full, down_full = (
        lax.all_gather(qkv_weight.astype(jnp.bfloat16), "dp", axis=0, tiled=True),
        lax.all_gather(out_weight.astype(jnp.bfloat16), "dp", axis=1, tiled=True),
        lax.all_gather(in_weight.astype(jnp.bfloat16), "dp", axis=0, tiled=True),
        lax.all_gather(down_weight.astype(jnp.bfloat16), "dp", axis=1, tiled=True),
    )
    model_dim = qkv_full.shape[0]
    head_dim = HD
    local_heads = qkv_full.shape[1] // (3 * head_dim)
    local_hidden = in_full.shape[2]
    head_feats = local_heads * head_dim
    in_flat = in_full.reshape(model_dim, 2 * local_hidden)
    first_token = lax.axis_index("dp") * seq_rows
    places = first_token + jnp.arange(seq_rows, dtype=jnp.int32)
    query_ids, offsets = seq_coords(seq_lengths, places)
    cos_table, sin_table = rotary_tables(offsets, head_dim)
    key_places = first_token - reach + jnp.arange(seq_rows + 2 * reach, dtype=jnp.int32)
    inside = (key_places >= 0) & (key_places < seq_rows * data_count)
    key_ids = jnp.where(inside, seq_coords(seq_lengths, key_places)[0], -1)
    first_normed, first_inv, first_scaled = norm_forward(residual_in, norm_gains[0])
    normed_in = lax.all_gather(first_scaled.astype(jnp.bfloat16), "tensor", axis=0, tiled=True)
    proj = jnp.dot(normed_in, qkv_full, preferred_element_type=jnp.float32).reshape(
        seq_rows, local_heads, 3, head_dim
    )
    queries = rotate(proj[:, :, 0], cos_table, sin_table).astype(jnp.bfloat16)
    keys = rotate(proj[:, :, 1], cos_table, sin_table).astype(jnp.bfloat16)
    values = proj[:, :, 2].astype(jnp.bfloat16)
    key_vals = jnp.concatenate(
        [keys.reshape(seq_rows, head_feats), values.reshape(seq_rows, head_feats)], axis=1
    )
    key_vals_pad = padded(key_vals, (("dp", 0),), reach)
    keys_pad = key_vals_pad[:, :head_feats].reshape(seq_rows + 2 * reach, local_heads, head_dim)
    values_pad = key_vals_pad[:, head_feats:].reshape(seq_rows + 2 * reach, local_heads, head_dim)
    allowed = block_mask(query_ids, key_ids, reach)
    mixed_part, norm_part = block_forward(queries, keys_pad, values_pad, allowed)
    mixed_flat = mixed_part.reshape(seq_rows, head_feats)
    attn_out = lax.psum_scatter(
        product_rows(mixed_flat, out_full, 0), "tensor", scatter_dimension=0, tiled=True
    )
    middle = residual_in + attn_out
    second_normed, second_inv, second_scaled = norm_forward(middle, norm_gains[1])
    ffn_in = lax.all_gather(second_scaled.astype(jnp.bfloat16), "tensor", axis=0, tiled=True)
    both = jnp.dot(ffn_in, in_flat, preferred_element_type=jnp.float32).reshape(
        seq_rows, 2, local_hidden
    )
    activated, slope = gelu_parts(both[:, 0])
    gated = (activated * both[:, 1]).astype(jnp.bfloat16)
    ffn_out = lax.psum_scatter(
        product_rows(gated, down_full, 0).astype(jnp.bfloat16),
        "tensor",
        scatter_dimension=0,
        tiled=True,
    ).astype(jnp.float32)
    block_out = middle + ffn_out
    grad_out_all = lax.all_gather(out_cotangent.astype(jnp.bfloat16), "tensor", axis=0, tiled=True)
    grad_gated = against_cols(grad_out_all, down_full)
    down_grad_part = across_rows(gated, grad_out_all)
    grad_both = jnp.stack([grad_gated * both[:, 1] * slope, grad_gated * activated], axis=1)
    grad_both_flat = grad_both.astype(jnp.bfloat16).reshape(seq_rows, 2 * local_hidden)
    in_grad_part = across_rows(ffn_in, grad_both_flat).reshape(model_dim, 2, local_hidden)
    grad_ffn_in = lax.psum_scatter(
        product_rows(grad_both_flat, in_flat, 1), "tensor", scatter_dimension=0, tiled=True
    )
    grad_second, second_gain_part = norm_backward(
        grad_ffn_in, second_normed, second_inv, norm_gains[1]
    )
    grad_middle = out_cotangent + grad_second
    middle_all = lax.all_gather(grad_middle.astype(jnp.bfloat16), "tensor", axis=0, tiled=True)
    out_grad_part = across_rows(mixed_flat, middle_all)
    grad_mixed = (
        against_cols(middle_all, out_full)
        .astype(jnp.bfloat16)
        .reshape(seq_rows, local_heads, head_dim)
    )
    deltas = jnp.sum(grad_mixed.astype(jnp.float32) * mixed_part.astype(jnp.float32), axis=-1)
    grad_kv_pad = jnp.zeros((seq_rows + 2 * reach, 2 * head_feats), jnp.float32)
    allowed = block_mask(query_ids, key_ids, reach)
    grad_q, grad_k, grad_v = block_backward(
        queries, keys_pad, values_pad, allowed, norm_part, grad_mixed, deltas
    )
    update = jnp.concatenate(
        [grad_k.reshape(span, head_feats), grad_v.reshape(span, head_feats)], axis=1
    )
    grad_kv_pad = grad_kv_pad.at[0:span].add(update)
    edge_grads = jnp.concatenate([grad_kv_pad[:reach], grad_kv_pad[seq_rows + reach :]], axis=0)
    edge_ext = padded(edge_grads.astype(jnp.bfloat16), (("dp", 0),), reach).astype(edge_grads.dtype)
    own_grads = grad_kv_pad[reach : reach + seq_rows]
    own_grads = own_grads.at[:reach].add(edge_ext[:reach])
    own_grads = own_grads.at[seq_rows - reach :].add(edge_ext[3 * reach :])
    grad_keys = own_grads[:, :head_feats].reshape(seq_rows, local_heads, head_dim)
    grad_values = own_grads[:, head_feats:].reshape(seq_rows, local_heads, head_dim)
    grad_proj = jnp.stack(
        [
            unrotate(grad_q, cos_table, sin_table),
            unrotate(grad_keys, cos_table, sin_table),
            grad_values,
        ],
        axis=2,
    )
    grad_proj_flat = grad_proj.astype(jnp.bfloat16).reshape(seq_rows, 3 * head_feats)
    qkv_grad_part = across_rows(normed_in, grad_proj_flat)
    grad_norm_in = lax.psum_scatter(
        product_rows(grad_proj_flat, qkv_full, 1).astype(jnp.bfloat16),
        "tensor",
        scatter_dimension=0,
        tiled=True,
    ).astype(jnp.float32)
    grad_first, first_gain_part = norm_backward(
        grad_norm_in, first_normed, first_inv, norm_gains[0]
    )
    residual_grad = grad_middle + grad_first
    gains_grad = lax.psum(jnp.stack([first_gain_part, second_gain_part]), ("dp", "tensor"))
    qkv_grad, out_weight_grad, in_grad, down_grad = (
        lax.psum_scatter(
            qkv_grad_part.astype(jnp.bfloat16), "dp", scatter_dimension=0, tiled=True
        ).astype(jnp.float32),
        lax.psum_scatter(
            out_grad_part.astype(jnp.bfloat16), "dp", scatter_dimension=1, tiled=True
        ).astype(jnp.float32),
        lax.psum_scatter(
            in_grad_part.astype(jnp.bfloat16), "dp", scatter_dimension=0, tiled=True
        ).astype(jnp.float32),
        lax.psum_scatter(
            down_grad_part.astype(jnp.bfloat16), "dp", scatter_dimension=1, tiled=True
        ).astype(jnp.float32),
    )
    new_qkv, new_qkv_moments = adam_update(qkv_weight, qkv_moments, qkv_grad, DECAY_RATE)
    new_out, new_out_moments = adam_update(out_weight, out_moments, out_weight_grad, DECAY_RATE)
    new_in, new_in_moments = adam_update(in_weight, in_moments, in_grad, DECAY_RATE)
    new_down, new_down_moments = adam_update(down_weight, down_moments, down_grad, DECAY_RATE)
    new_gains, new_gain_moments = adam_update(norm_gains, gain_moments, gains_grad, 0.0)
    return (
        block_out,
        residual_grad,
        qkv_grad,
        out_weight_grad,
        in_grad,
        down_grad,
        gains_grad,
        new_qkv,
        new_out,
        new_in,
        new_down,
        new_gains,
        new_qkv_moments,
        new_out_moments,
        new_in_moments,
        new_down_moments,
        new_gain_moments,
    )


def solution(mesh):
    return jax.shard_map(
        local,
        mesh=mesh,
        in_specs=(
            P(("dp", "tensor"), None),
            P(("dp", "tensor"), None),
            P(),
            P("dp", "tensor"),
            P("tensor", "dp"),
            P("dp", None, "tensor"),
            P("tensor", "dp"),
            P(),
            P(None, "dp", "tensor"),
            P(None, "tensor", "dp"),
            P(None, "dp", None, "tensor"),
            P(None, "tensor", "dp"),
            P(),
        ),
        out_specs=(
            P(("dp", "tensor"), None),
            P(("dp", "tensor"), None),
            P("dp", "tensor"),
            P("tensor", "dp"),
            P("dp", None, "tensor"),
            P("tensor", "dp"),
            P(),
            P("dp", "tensor"),
            P("tensor", "dp"),
            P("dp", None, "tensor"),
            P("tensor", "dp"),
            P(),
            P(None, "dp", "tensor"),
            P(None, "tensor", "dp"),
            P(None, "dp", None, "tensor"),
            P(None, "tensor", "dp"),
            P(),
        ),
        check_vma=False,
    )
```

profile of v0, /device:TPU:0, one launch (start us, length us, event | category | flops | bytes accessed | tf_op | source)
XLA Modules:
  0.0 752.0 jit_solution(12880494471490557528)
XLA Ops:
  15.8 20.5 %all-gather.9.cloned.1.call-done = bf16[512,1024]{1,0:T(8,128)(2,1)} async-done(((bf16[256,1024]{1,0:T(8,128)(2,1)}), bf16[512,1024]{1,0:T(8,128)(2,1)}) %all-gather.9.cloned.1.call-update) | async-done | bytes 1048592 | tf_op jit(solution)/shard_map/all_gather | solution.py:215
  36.2 48.3 %all-gather.11.cloned.1.call-done = bf16[1024,1536]{1,0:T(8,128)(2,1)} async-done(((bf16[64,1536]{1,0:T(8,128)(2,1)}), bf16[1024,1536]{1,0:T(8,128)(2,1)}) %all-gather.11.cloned.1.call-update) | async-done | bytes 3145744 | tf_op jit(solution)/shard_map/all_gather | solution.py:196
  106.3 18.5 %all-gather.13.cloned.1.call-done = bf16[512,1024]{0,1:T(8,128)(2,1)} async-done(((bf16[512,64]{0,1:T(8,128)(2,1)}), bf16[512,1024]{0,1:T(8,128)(2,1)}) %all-gather.13.cloned.1.call-update) | async-done | bytes 1048592 | tf_op jit(solution)/shard_map/all_gather | solution.py:197
  129.3 29.9 %reduce-scatter.9.cloned.1.call-done = f32[256,1024]{1,0:T(8,128)} async-done(((f32[512,1024]{1,0:T(8,128)}), f32[256,1024]{1,0:T(8,128)}) %reduce-scatter.9.cloned.1.call-update) | async-done | bytes 1048592 | tf_op jit(solution)/shard_map/reduce_scatter | solution.py:231
  163.0 57.7 %all-gather.17.cloned.1.call-done = bf16[1024,2,1312]{2,0,1:T(8,128)(2,1)} async-done(((bf16[64,2,1312]{2,0,1:T(8,128)(2,1)}), bf16[1024,2,1312]{2,0,1:T(8,128)(2,1)}) %all-gather.17.cloned.1.call-update) | async-done | bytes 5373968 | tf_op jit(solution)/shard_map/all_gather | solution.py:198
  220.7 8.1 %copy.60 = bf16[1024,2,1312]{0,2,1:T(8,128)(2,1)} copy(bf16[1024,2,1312]{2,0,1:T(8,128)(2,1)} %all-gather.17.cloned.1.call-done) | data formatting | bytes 10747904 | tf_op jit(solution)/shard_map/all_gather | solution.py:198
  228.8 13.8 %all-gather.15.cloned.1.call-done = bf16[512,1024]{1,0:T(8,128)(2,1)} async-done(((bf16[256,1024]{1,0:T(8,128)(2,1)}), bf16[512,1024]{1,0:T(8,128)(2,1)}) %all-gather.15.cloned.1.call-update) | async-done | bytes 1048592 | tf_op jit(solution)/shard_map/all_gather | solution.py:236
  242.6 5.3 fusion.2
  252.0 14.1 %all-gather.21.cloned.1.call-done = bf16[512,1024]{1,0:T(8,128)(2,1)} async-done(((bf16[256,1024]{1,0:T(8,128)(2,1)}), bf16[512,1024]{1,0:T(8,128)(2,1)}) %all-gather.21.cloned.1.call-update) | async-done | bytes 1048592 | tf_op jit(solution)/shard_map/all_gather | solution.py:249
  271.2 65.3 %reduce-scatter.23.cloned.1.call-done = bf16[1312,64]{0,1:T(8,128)(2,1)} async-done(((bf16[1312,1024]{0,1:T(8,128)(2,1)}), bf16[1312,64]{0,1:T(8,128)(2,1)}) %reduce-scatter.23.cloned.1.call-update) | async-done | bytes 167952 | tf_op jit(solution)/shard_map/reduce_scatter | solution.py:317
  341.7 43.1 %all-gather.19.cloned.1.call-done = bf16[1312,1024]{0,1:T(8,128)(2,1)} async-done(((bf16[1312,64]{0,1:T(8,128)(2,1)}), bf16[1312,1024]{0,1:T(8,128)(2,1)}) %all-gather.19.cloned.1.call-update) | async-done | bytes 2686992 | tf_op jit(solution)/shard_map/all_gather | solution.py:199
  384.8 6.5 fusion.9
  392.7 7.2 convolution_bitcast_fusion
  405.3 25.3 %reduce-scatter.13.cloned.1.call-done = f32[256,1024]{1,0:T(8,128)} async-done(((f32[512,1024]{1,0:T(8,128)}), f32[256,1024]{1,0:T(8,128)}) %reduce-scatter.13.cloned.1.call-update) | async-done | bytes 1048592 | tf_op jit(solution)/shard_map/reduce_scatter | solution.py:255
  432.9 20.9 %reduce-scatter.11.cloned.1.call-done = bf16[256,1024]{1,0:T(8,128)(2,1)} async-done(((bf16[512,1024]{1,0:T(8,128)(2,1)}), bf16[256,1024]{1,0:T(8,128)(2,1)}) %reduce-scatter.11.cloned.1.call-update) | async-done | bytes 524304 | tf_op jit(solution)/shard_map/reduce_scatter | solution.py:242
  457.3 21.4 %all-gather.23.cloned.1.call-done = bf16[512,1024]{1,0:T(8,128)(2,1)} async-done(((bf16[256,1024]{1,0:T(8,128)(2,1)}), bf16[512,1024]{1,0:T(8,128)(2,1)}) %all-gather.23.cloned.1.call-update) | async-done | bytes 1048592 | tf_op jit(solution)/shard_map/all_gather | solution.py:262
  481.1 5.6 fusion.57
  486.8 6.7 multiply_convert_fusion
  529.8 6.4 convolution_convert_fusion
  545.8 19.0 %reduce-scatter.19.cloned.1.call-done = bf16[512,64]{0,1:T(8,128)(2,1)} async-done(((bf16[512,1024]{0,1:T(8,128)(2,1)}), bf16[512,64]{0,1:T(8,128)(2,1)}) %reduce-scatter.19.cloned.1.call-update) | async-done | bytes 65552 | tf_op jit(solution)/shard_map/reduce_scatter | solution.py:311
  568.3 18.6 %reduce-scatter.15.cloned.1.call-done = bf16[256,1024]{1,0:T(8,128)(2,1)} async-done(((bf16[512,1024]{1,0:T(8,128)(2,1)}), bf16[256,1024]{1,0:T(8,128)(2,1)}) %reduce-scatter.15.cloned.1.call-update) | async-done | bytes 524304 | tf_op jit(solution)/shard_map/reduce_scatter | solution.py:296
  590.3 40.4 %psum.7 = f32[2,1024]{1,0:T(2,128)} all-reduce(f32[2,1024]{1,0:T(2,128)} %pad_maximum_fusion.12), channel_id=1, replica_groups=mesh['dp'=16,'tensor'=2] {'dp','tensor'}, use_global_device_ids=true, to_apply=%region_25.26 | all-reduce | flops 2048 | bytes 16384 | tf_op jit(solution)/shard_map/psum | solution.py:306
  636.4 36.2 %reduce-scatter.21.cloned.1.call-done = bf16[64,2,1312]{2,0,1:T(8,128)(2,1)} async-done(((bf16[1024,2,1312]{2,0,1:T(8,128)(2,1)}), bf16[64,2,1312]{2,0,1:T(8,128)(2,1)}) %reduce-scatter.21.cloned.1.call-update) | async-done | bytes 335888 | tf_op jit(solution)/shard_map/reduce_scatter | solution.py:314
  679.5 62.4 %reduce-scatter.17.cloned.1.call-done = bf16[64,1536]{1,0:T(8,128)(2,1)} async-done(((bf16[1024,1536]{1,0:T(8,128)(2,1)}), bf16[64,1536]{1,0:T(8,128)(2,1)}) %reduce-scatter.17.cloned.1.call-update) | async-done | bytes 196624 | tf_op jit(solution)/shard_map/reduce_scatter | solution.py:308
  (225 shorter events, 135.3 us)
Async XLA Ops:
  7.2 29.0 %all-gather.9.cloned.1.call-start = ((), (), s32[]{:S(2)}) async-start(), calls=%async_computation.8 | async-start | bytes 1572864 | tf_op jit(solution)/shard_map/all_gather | solution.py:215
  10.2 78.4 %copy-start.37 = (f32[256]{0:T(256)}, f32[256]{0:T(256)S(1)}, u32[]{:S(2)}) copy-start(f32[256]{0:T(256)S(1)} %add_rsqrt_fusion.1) | copy-start | bytes 3076
  12.1 72.5 %all-gather.11.cloned.1.call-start = ((), (), s32[]{:S(2)}) async-start(), calls=%async_computation.9 | async-start | bytes 3342336 | tf_op jit(solution)/shard_map/all_gather | solution.py:196
  12.9 112.0 %all-gather.13.cloned.1.call-start = ((), (), s32[]{:S(2)}) async-start(), calls=%async_computation.10 | async-start | bytes 1114112 | tf_op jit(solution)/shard_map/all_gather | solution.py:197
  13.6 145.7 %reduce-scatter.9.cloned.1.call-start = ((), (), s32[]{:S(2)}) async-start(), calls=%async_computation.11 | async-start | bytes 3145728 | tf_op jit(solution)/shard_map/reduce_scatter | solution.py:231
  90.3 3.9 collective-permute-start
  92.4 3.4 collective-permute-start.1
  128.2 92.5 %all-gather.17.cloned.1.call-start = ((), (), s32[]{:S(2)}) async-start(), calls=%async_computation.13 | async-start | bytes 6127616 | tf_op jit(solution)/shard_map/all_gather | solution.py:198
  129.3 113.3 %all-gather.15.cloned.1.call-start = ((), (), s32[]{:S(2)}) async-start(), calls=%async_computation.12 | async-start | bytes 1572864 | tf_op jit(solution)/shard_map/all_gather | solution.py:236
  162.0 104.1 %all-gather.21.cloned.1.call-start = ((), (), s32[]{:S(2)}) async-start(), calls=%async_computation.16 | async-start | bytes 1572864 | tf_op jit(solution)/shard_map/all_gather | solution.py:249
  162.9 173.6 %reduce-scatter.23.cloned.1.call-start = ((), (), s32[]{:S(2)}) async-start(), calls=%async_computation.23 | async-start | bytes 3063808 | tf_op jit(solution)/shard_map/reduce_scatter | solution.py:317
  271.2 113.6 %all-gather.19.cloned.1.call-start = ((), (), s32[]{:S(2)}) async-start(), calls=%async_computation.14 | async-start | bytes 3063808 | tf_op jit(solution)/shard_map/all_gather | solution.py:199
  341.6 89.0 %reduce-scatter.13.cloned.1.call-start = ((), (), s32[]{:S(2)}) async-start(), calls=%async_computation.17 | async-start | bytes 3145728 | tf_op jit(solution)/shard_map/reduce_scatter | solution.py:255
  400.0 53.9 %reduce-scatter.11.cloned.1.call-start = ((), (), s32[]{:S(2)}) async-start(), calls=%async_computation.15 | async-start | bytes 1572864 | tf_op jit(solution)/shard_map/reduce_scatter | solution.py:242
  405.3 73.4 %all-gather.23.cloned.1.call-start = ((), (), s32[]{:S(2)}) async-start(), calls=%async_computation.18 | async-start | bytes 1572864 | tf_op jit(solution)/shard_map/all_gather | solution.py:262
  457.2 107.5 %reduce-scatter.19.cloned.1.call-start = ((), (), s32[]{:S(2)}) async-start(), calls=%async_computation.21 | async-start | bytes 1114112 | tf_op jit(solution)/shard_map/reduce_scatter | solution.py:311
  499.5 10.1 %collective-permute-start.2 = (bf16[64,1024]{0,1:T(8,128)(2,1)}, bf16[64,1024]{0,1:T(8,128)(2,1)}, u32[]{:S(2)}, u32[]{:S(2)}) collective-permute-start(bf16[64,1024]{0,1:T(8,128)(2,1)} %get-tuple-element.137), channel_id=1, source_target_pairs={{0,2},{2,4},{4,6},{6,8},{8,10},{10,12},{12,14},{14,16},{16,18},{18... | collective-permute-start | bytes 393224 | tf_op jit(solution)/shard_map/ppermute | solution.py:27
  501.8 7.8 %collective-permute-start.3 = (bf16[64,1024]{0,1:T(8,128)(2,1)}, bf16[64,1024]{0,1:T(8,128)(2,1)}, u32[]{:S(2)}, u32[]{:S(2)}) collective-permute-start(bf16[64,1024]{0,1:T(8,128)(2,1)} %get-tuple-element.138), channel_id=1, source_target_pairs={{2,0},{4,2},{6,4},{8,6},{10,8},{12,10},{14,12},{16,14},{18,16},{20... | collective-permute-start | bytes 393224 | tf_op jit(solution)/shard_map/ppermute | solution.py:28
  505.0 81.9 %reduce-scatter.15.cloned.1.call-start = ((), (), s32[]{:S(2)}) async-start(), calls=%async_computation.19 | async-start | bytes 1572864 | tf_op jit(solution)/shard_map/reduce_scatter | solution.py:296
  529.7 142.9 %reduce-scatter.21.cloned.1.call-start = ((), (), s32[]{:S(2)}) async-start(), calls=%async_computation.22 | async-start | bytes 6127616 | tf_op jit(solution)/shard_map/reduce_scatter | solution.py:314
  536.2 205.7 %reduce-scatter.17.cloned.1.call-start = ((), (), s32[]{:S(2)}) async-start(), calls=%async_computation.20 | async-start | bytes 3342336 | tf_op jit(solution)/shard_map/reduce_scatter | solution.py:308
  544.9 85.8 %copy-start.36 = (f32[2,1024]{1,0:T(2,128)S(1)}, f32[2,1024]{1,0:T(2,128)}, u32[]{:S(2)}) copy-start(f32[2,1024]{1,0:T(2,128)} %param.28) | copy-start | bytes 24580
  544.9 89.2 %copy-start.9 = (f32[256,1024]{1,0:T(8,128)S(1)}, f32[256,1024]{1,0:T(8,128)}, u32[]{:S(2)}) copy-start(f32[256,1024]{1,0:T(8,128)} %get-tuple-element.127) | copy-start | bytes 3145732
  568.3 104.4 %copy-start.13 = (f32[64,2,1312]{2,1,0:T(2,128)S(1)}, f32[64,2,1312]{2,1,0:T(2,128)}, u32[]{:S(2)}) copy-start(f32[64,2,1312]{2,1,0:T(2,128)} %param.26) | copy-start | bytes 2015236
  (42 other events, 472.3 us)
Sparse Core Ops, SparseCore 0:
  12.2 23.9 all-gather.8
  39.1 45.4 all-gather.10
  87.3 37.4 all-gather.12
  128.4 30.8 reduce-scatter.8
  162.0 58.6 all-gather.16
  222.7 19.9 all-gather.14
  244.7 21.2 all-gather.20
  271.3 65.1 reduce-scatter.22
  341.7 42.9 all-gather.18
  400.1 30.5 reduce-scatter.12
  433.5 20.3 reduce-scatter.10
  457.3 21.2 all-gather.22
  505.1 59.6 reduce-scatter.18
  567.4 19.3 reduce-scatter.14
  590.6 82.0 reduce-scatter.20
  676.3 65.5 reduce-scatter.16
where the time goes:
time: 762 us; the launch traced here: 752 us
  waiting for transfers between devices  517 us (68%)
  matrix products  76.6 us (10%)
  other arithmetic  56 us (7%)
  blocking collectives  40.4 us (5%)
  local copies, waits for them, and re-layouts  38.4 us (5%)
  between operations  15.2 us (2%)
  starting transfers between devices  8.29 us (1%)
    reduce_scatter x1, waiting for transfers between devices, local(): lax.psum_scatter(down_grad_part.astype(jnp.bfloat16), 'dp', scatter_dimen...  65.3 us
    reduce_scatter x1, waiting for transfers between devices, local(): lax.psum_scatter(qkv_grad_part.astype(jnp.bfloat16), 'dp', scatter_dimens...  62.4 us
    all_gather x1, waiting for transfers between devices, local(): lax.all_gather(in_weight.astype(jnp.bfloat16), 'dp', axis=0, tiled=True)  57.7 us
    all_gather x1, waiting for transfers between devices, local(): lax.all_gather(qkv_weight.astype(jnp.bfloat16), 'dp', axis=0, tiled=True)  48.3 us
    all_gather x1, waiting for transfers between devices, local(): lax.all_gather(down_weight.astype(jnp.bfloat16), 'dp', axis=1, tiled=True)  43.1 us
    psum x1, blocking collectives, local(): lax.psum(jnp.stack([first_gain_part, second_gain_part]), ('dp', 'tensor'))  40.4 us
    reduce_scatter x1, waiting for transfers between devices, local(): lax.psum_scatter(in_grad_part.astype(jnp.bfloat16), 'dp', scatter_dimensi...  36.2 us
    reduce_scatter x1, waiting for transfers between devices, local(): lax.psum_scatter(product_rows(mixed_flat, out_full, 0), 'tensor', scatter...  29.9 us
  transfers between devices with their start and end apart: 20, of which 17 were waited for; matrix products, arithmetic and copies ran while one was open for 14% of the time, Pallas kernels for 0%

commit v1 on v0

--- a/solution.py
+++ b/solution.py
@@ -303,7 +303,7 @@
         grad_norm_in, first_normed, first_inv, norm_gains[0]
     )
     residual_grad = grad_middle + grad_first
-    gains_grad = lax.psum(jnp.stack([first_gain_part, second_gain_part]), ("dp", "tensor"))
+    gains_grad = lax.psum(lax.psum(jnp.stack([first_gain_part, second_gain_part]), "dp"), "tensor")
     qkv_grad, out_weight_grad, in_grad, down_grad = (
         lax.psum_scatter(
             qkv_grad_part.astype(jnp.bfloat16), "dp", scatter_dimension=0, tiled=True

time: 762 us -> 761 us (level)
    psum x1 -> x2, blocking collectives: 40.4 us -> 40.2 us  [the longest x1 34.3 us: local(): lax.psum(jnp.stack([first_gain_part, second_gain_part]), 'dp')]
where the time goes in v1:
time: 761 us; the launch traced here: 751 us
  waiting for transfers between devices  517 us (68%)
  matrix products  76.6 us (10%)
  other arithmetic  56 us (7%)
  blocking collectives  40.2 us (5%)
  local copies, waits for them, and re-layouts  38.4 us (5%)
  between operations  15.3 us (2%)
  starting transfers between devices  8.29 us (1%)
    reduce_scatter x1, waiting for transfers between devices, local(): lax.psum_scatter(down_grad_part.astype(jnp.bfloat16), 'dp', scatter_dimen...  65.3 us
    reduce_scatter x1, waiting for transfers between devices, local(): lax.psum_scatter(qkv_grad_part.astype(jnp.bfloat16), 'dp', scatter_dimens...  62.5 us
    all_gather x1, waiting for transfers between devices, local(): lax.all_gather(in_weight.astype(jnp.bfloat16), 'dp', axis=0, tiled=True)  57.7 us
    all_gather x1, waiting for transfers between devices, local(): lax.all_gather(qkv_weight.astype(jnp.bfloat16), 'dp', axis=0, tiled=True)  48.3 us
    all_gather x1, waiting for transfers between devices, local(): lax.all_gather(down_weight.astype(jnp.bfloat16), 'dp', axis=1, tiled=True)  43.1 us
    reduce_scatter x1, waiting for transfers between devices, local(): lax.psum_scatter(in_grad_part.astype(jnp.bfloat16), 'dp', scatter_dimensi...  35.8 us
    psum x1, blocking collectives, local(): lax.psum(jnp.stack([first_gain_part, second_gain_part]), 'dp')  34.3 us
    reduce_scatter x1, waiting for transfers between devices, local(): lax.psum_scatter(product_rows(mixed_flat, out_full, 0), 'tensor', scatter...  29.9 us
  transfers between devices with their start and end apart: 20, of which 17 were waited for; matrix products, arithmetic and copies ran while one was open for 14% of the time, Pallas kernels for 0%

profile of v1, /device:TPU:0, one launch (start us, length us, event | category | flops | bytes accessed | tf_op | source)
XLA Modules:
  0.0 751.3 jit_solution(10555810147841030355)
XLA Ops:
  15.8 20.5 %all-gather.9.cloned.1.call-done = bf16[512,1024]{1,0:T(8,128)(2,1)} async-done(((bf16[256,1024]{1,0:T(8,128)(2,1)}), bf16[512,1024]{1,0:T(8,128)(2,1)}) %all-gather.9.cloned.1.call-update) | async-done | bytes 1048592 | tf_op jit(solution)/shard_map/all_gather | solution.py:215
  36.2 48.3 %all-gather.11.cloned.1.call-done = bf16[1024,1536]{1,0:T(8,128)(2,1)} async-done(((bf16[64,1536]{1,0:T(8,128)(2,1)}), bf16[1024,1536]{1,0:T(8,128)(2,1)}) %all-gather.11.cloned.1.call-update) | async-done | bytes 3145744 | tf_op jit(solution)/shard_map/all_gather | solution.py:196
  106.2 18.6 %all-gather.13.cloned.1.call-done = bf16[512,1024]{0,1:T(8,128)(2,1)} async-done(((bf16[512,64]{0,1:T(8,128)(2,1)}), bf16[512,1024]{0,1:T(8,128)(2,1)}) %all-gather.13.cloned.1.call-update) | async-done | bytes 1048592 | tf_op jit(solution)/shard_map/all_gather | solution.py:197
  129.3 29.9 %reduce-scatter.9.cloned.1.call-done = f32[256,1024]{1,0:T(8,128)} async-done(((f32[512,1024]{1,0:T(8,128)}), f32[256,1024]{1,0:T(8,128)}) %reduce-scatter.9.cloned.1.call-update) | async-done | bytes 1048592 | tf_op jit(solution)/shard_map/reduce_scatter | solution.py:231
  163.0 57.7 %all-gather.17.cloned.1.call-done = bf16[1024,2,1312]{2,0,1:T(8,128)(2,1)} async-done(((bf16[64,2,1312]{2,0,1:T(8,128)(2,1)}), bf16[1024,2,1312]{2,0,1:T(8,128)(2,1)}) %all-gather.17.cloned.1.call-update) | async-done | bytes 5373968 | tf_op jit(solution)/shard_map/all_gather | solution.py:198
  220.7 8.1 %copy.60 = bf16[1024,2,1312]{0,2,1:T(8,128)(2,1)} copy(bf16[1024,2,1312]{2,0,1:T(8,128)(2,1)} %all-gather.17.cloned.1.call-done) | data formatting | bytes 10747904 | tf_op jit(solution)/shard_map/all_gather | solution.py:198
  228.8 13.8 %all-gather.15.cloned.1.call-done = bf16[512,1024]{1,0:T(8,128)(2,1)} async-done(((bf16[256,1024]{1,0:T(8,128)(2,1)}), bf16[512,1024]{1,0:T(8,128)(2,1)}) %all-gather.15.cloned.1.call-update) | async-done | bytes 1048592 | tf_op jit(solution)/shard_map/all_gather | solution.py:236
  252.0 14.1 %all-gather.21.cloned.1.call-done = bf16[512,1024]{1,0:T(8,128)(2,1)} async-done(((bf16[256,1024]{1,0:T(8,128)(2,1)}), bf16[512,1024]{1,0:T(8,128)(2,1)}) %all-gather.21.cloned.1.call-update) | async-done | bytes 1048592 | tf_op jit(solution)/shard_map/all_gather | solution.py:249
  271.2 65.3 %reduce-scatter.23.cloned.1.call-done = bf16[1312,64]{0,1:T(8,128)(2,1)} async-done(((bf16[1312,1024]{0,1:T(8,128)(2,1)}), bf16[1312,64]{0,1:T(8,128)(2,1)}) %reduce-scatter.23.cloned.1.call-update) | async-done | bytes 167952 | tf_op jit(solution)/shard_map/reduce_scatter | solution.py:317
  341.7 43.1 %all-gather.19.cloned.1.call-done = bf16[1312,1024]{0,1:T(8,128)(2,1)} async-done(((bf16[1312,64]{0,1:T(8,128)(2,1)}), bf16[1312,1024]{0,1:T(8,128)(2,1)}) %all-gather.19.cloned.1.call-update) | async-done | bytes 2686992 | tf_op jit(solution)/shard_map/all_gather | solution.py:199
  384.7 6.5 fusion.9
  392.7 7.2 convolution_bitcast_fusion
  405.3 25.3 %reduce-scatter.13.cloned.1.call-done = f32[256,1024]{1,0:T(8,128)} async-done(((f32[512,1024]{1,0:T(8,128)}), f32[256,1024]{1,0:T(8,128)}) %reduce-scatter.13.cloned.1.call-update) | async-done | bytes 1048592 | tf_op jit(solution)/shard_map/reduce_scatter | solution.py:255
  432.9 20.9 %reduce-scatter.11.cloned.1.call-done = bf16[256,1024]{1,0:T(8,128)(2,1)} async-done(((bf16[512,1024]{1,0:T(8,128)(2,1)}), bf16[256,1024]{1,0:T(8,128)(2,1)}) %reduce-scatter.11.cloned.1.call-update) | async-done | bytes 524304 | tf_op jit(solution)/shard_map/reduce_scatter | solution.py:242
  457.2 21.4 %all-gather.23.cloned.1.call-done = bf16[512,1024]{1,0:T(8,128)(2,1)} async-done(((bf16[256,1024]{1,0:T(8,128)(2,1)}), bf16[512,1024]{1,0:T(8,128)(2,1)}) %all-gather.23.cloned.1.call-update) | async-done | bytes 1048592 | tf_op jit(solution)/shard_map/all_gather | solution.py:262
  481.1 5.6 fusion.57
  486.8 6.7 multiply_convert_fusion
  529.8 6.4 convolution_convert_fusion
  545.8 18.9 %reduce-scatter.19.cloned.1.call-done = bf16[512,64]{0,1:T(8,128)(2,1)} async-done(((bf16[512,1024]{0,1:T(8,128)(2,1)}), bf16[512,64]{0,1:T(8,128)(2,1)}) %reduce-scatter.19.cloned.1.call-update) | async-done | bytes 65552 | tf_op jit(solution)/shard_map/reduce_scatter | solution.py:311
  568.2 18.6 %reduce-scatter.15.cloned.1.call-done = bf16[256,1024]{1,0:T(8,128)(2,1)} async-done(((bf16[512,1024]{1,0:T(8,128)(2,1)}), bf16[256,1024]{1,0:T(8,128)(2,1)}) %reduce-scatter.15.cloned.1.call-update) | async-done | bytes 524304 | tf_op jit(solution)/shard_map/reduce_scatter | solution.py:296
  590.2 34.3 %psum.14 = f32[2,1024]{1,0:T(2,128)} all-reduce(f32[2,1024]{1,0:T(2,128)} %pad_maximum_fusion.12), channel_id=1, replica_groups=mesh['dp'=16,'tensor'=2] {'dp'}, use_global_device_ids=true, to_apply=%region_25.26 | all-reduce | flops 2048 | bytes 16384 | tf_op jit(solution)/shard_map/psum | solution.py:306
  624.5 6.0 psum.15
  636.2 35.8 %reduce-scatter.21.cloned.1.call-done = bf16[64,2,1312]{2,0,1:T(8,128)(2,1)} async-done(((bf16[1024,2,1312]{2,0,1:T(8,128)(2,1)}), bf16[64,2,1312]{2,0,1:T(8,128)(2,1)}) %reduce-scatter.21.cloned.1.call-update) | async-done | bytes 335888 | tf_op jit(solution)/shard_map/reduce_scatter | solution.py:314
  678.8 62.5 %reduce-scatter.17.cloned.1.call-done = bf16[64,1536]{1,0:T(8,128)(2,1)} async-done(((bf16[1024,1536]{1,0:T(8,128)(2,1)}), bf16[64,1536]{1,0:T(8,128)(2,1)}) %reduce-scatter.17.cloned.1.call-update) | async-done | bytes 196624 | tf_op jit(solution)/shard_map/reduce_scatter | solution.py:308
  (226 shorter events, 140.6 us)
Async XLA Ops:
  7.2 29.0 %all-gather.9.cloned.1.call-start = ((), (), s32[]{:S(2)}) async-start(), calls=%async_computation.8 | async-start | bytes 1572864 | tf_op jit(solution)/shard_map/all_gather | solution.py:215
  10.2 78.4 %copy-start.37 = (f32[256]{0:T(256)}, f32[256]{0:T(256)S(1)}, u32[]{:S(2)}) copy-start(f32[256]{0:T(256)S(1)} %add_rsqrt_fusion.1) | copy-start | bytes 3076
  12.1 72.5 %all-gather.11.cloned.1.call-start = ((), (), s32[]{:S(2)}) async-start(), calls=%async_computation.9 | async-start | bytes 3342336 | tf_op jit(solution)/shard_map/all_gather | solution.py:196
  12.9 112.0 %all-gather.13.cloned.1.call-start = ((), (), s32[]{:S(2)}) async-start(), calls=%async_computation.10 | async-start | bytes 1114112 | tf_op jit(solution)/shard_map/all_gather | solution.py:197
  13.6 145.7 %reduce-scatter.9.cloned.1.call-start = ((), (), s32[]{:S(2)}) async-start(), calls=%async_computation.11 | async-start | bytes 3145728 | tf_op jit(solution)/shard_map/reduce_scatter | solution.py:231
  90.3 3.9 collective-permute-start
  92.4 3.4 collective-permute-start.1
  128.2 92.5 %all-gather.17.cloned.1.call-start = ((), (), s32[]{:S(2)}) async-start(), calls=%async_computation.13 | async-start | bytes 6127616 | tf_op jit(solution)/shard_map/all_gather | solution.py:198
  129.3 113.3 %all-gather.15.cloned.1.call-start = ((), (), s32[]{:S(2)}) async-start(), calls=%async_computation.12 | async-start | bytes 1572864 | tf_op jit(solution)/shard_map/all_gather | solution.py:236
  162.0 104.1 %all-gather.21.cloned.1.call-start = ((), (), s32[]{:S(2)}) async-start(), calls=%async_computation.16 | async-start | bytes 1572864 | tf_op jit(solution)/shard_map/all_gather | solution.py:249
  162.9 173.6 %reduce-scatter.23.cloned.1.call-start = ((), (), s32[]{:S(2)}) async-start(), calls=%async_computation.23 | async-start | bytes 3063808 | tf_op jit(solution)/shard_map/reduce_scatter | solution.py:317
  271.2 113.6 %all-gather.19.cloned.1.call-start = ((), (), s32[]{:S(2)}) async-start(), calls=%async_computation.14 | async-start | bytes 3063808 | tf_op jit(solution)/shard_map/all_gather | solution.py:199
  341.6 89.0 %reduce-scatter.13.cloned.1.call-start = ((), (), s32[]{:S(2)}) async-start(), calls=%async_computation.17 | async-start | bytes 3145728 | tf_op jit(solution)/shard_map/reduce_scatter | solution.py:255
  399.9 53.9 %reduce-scatter.11.cloned.1.call-start = ((), (), s32[]{:S(2)}) async-start(), calls=%async_computation.15 | async-start | bytes 1572864 | tf_op jit(solution)/shard_map/reduce_scatter | solution.py:242
  405.3 73.4 %all-gather.23.cloned.1.call-start = ((), (), s32[]{:S(2)}) async-start(), calls=%async_computation.18 | async-start | bytes 1572864 | tf_op jit(solution)/shard_map/all_gather | solution.py:262
  457.2 107.5 %reduce-scatter.19.cloned.1.call-start = ((), (), s32[]{:S(2)}) async-start(), calls=%async_computation.21 | async-start | bytes 1114112 | tf_op jit(solution)/shard_map/reduce_scatter | solution.py:311
  499.5 10.1 %collective-permute-start.2 = (bf16[64,1024]{0,1:T(8,128)(2,1)}, bf16[64,1024]{0,1:T(8,128)(2,1)}, u32[]{:S(2)}, u32[]{:S(2)}) collective-permute-start(bf16[64,1024]{0,1:T(8,128)(2,1)} %get-tuple-element.137), channel_id=1, source_target_pairs={{0,2},{2,4},{4,6},{6,8},{8,10},{10,12},{12,14},{14,16},{16,18},{18... | collective-permute-start | bytes 393224 | tf_op jit(solution)/shard_map/ppermute | solution.py:27
  501.8 7.8 %collective-permute-start.3 = (bf16[64,1024]{0,1:T(8,128)(2,1)}, bf16[64,1024]{0,1:T(8,128)(2,1)}, u32[]{:S(2)}, u32[]{:S(2)}) collective-permute-start(bf16[64,1024]{0,1:T(8,128)(2,1)} %get-tuple-element.138), channel_id=1, source_target_pairs={{2,0},{4,2},{6,4},{8,6},{10,8},{12,10},{14,12},{16,14},{18,16},{20... | collective-permute-start | bytes 393224 | tf_op jit(solution)/shard_map/ppermute | solution.py:28
  504.9 81.9 %reduce-scatter.15.cloned.1.call-start = ((), (), s32[]{:S(2)}) async-start(), calls=%async_computation.19 | async-start | bytes 1572864 | tf_op jit(solution)/shard_map/reduce_scatter | solution.py:296
  529.7 142.3 %reduce-scatter.21.cloned.1.call-start = ((), (), s32[]{:S(2)}) async-start(), calls=%async_computation.22 | async-start | bytes 6127616 | tf_op jit(solution)/shard_map/reduce_scatter | solution.py:314
  536.2 205.0 %reduce-scatter.17.cloned.1.call-start = ((), (), s32[]{:S(2)}) async-start(), calls=%async_computation.20 | async-start | bytes 3342336 | tf_op jit(solution)/shard_map/reduce_scatter | solution.py:308
  544.8 85.6 %copy-start.36 = (f32[2,1024]{1,0:T(2,128)S(1)}, f32[2,1024]{1,0:T(2,128)}, u32[]{:S(2)}) copy-start(f32[2,1024]{1,0:T(2,128)} %param.28) | copy-start | bytes 24580
  544.8 89.0 %copy-start.9 = (f32[256,1024]{1,0:T(8,128)S(1)}, f32[256,1024]{1,0:T(8,128)}, u32[]{:S(2)}) copy-start(f32[256,1024]{1,0:T(8,128)} %get-tuple-element.127) | copy-start | bytes 3145732
  568.2 103.8 %copy-start.13 = (f32[64,2,1312]{2,1,0:T(2,128)S(1)}, f32[64,2,1312]{2,1,0:T(2,128)}, u32[]{:S(2)}) copy-start(f32[64,2,1312]{2,1,0:T(2,128)} %param.26) | copy-start | bytes 2015236
  (42 other events, 472.3 us)
Sparse Core Ops, SparseCore 0:
  12.2 23.9 all-gather.8
  39.1 45.4 all-gather.10
  87.3 37.4 all-gather.12
  128.3 30.8 reduce-scatter.8
  161.9 58.6 all-gather.16
  222.7 19.8 all-gather.14
  244.7 21.2 all-gather.20
  271.3 65.1 reduce-scatter.22
  341.7 42.9 all-gather.18
  400.0 30.5 reduce-scatter.12
  433.4 20.3 reduce-scatter.10
  457.3 21.2 all-gather.22
  505.0 59.5 reduce-scatter.18
  567.3 19.4 reduce-scatter.14
  590.6 81.3 reduce-scatter.20
  675.7 65.5 reduce-scatter.16
